TPU v7x, 128 devices: a whole 4x4x4 slice. The times are simulated.
128 devices in a mesh: beam: 16 (over x_lo, y, core), seg: 8 (over z, x_hi).
Axes of the slice: x: 4 (x_hi: 2, x_lo: 2; x = x_hi * 2 + x_lo), y: 4, z: 4, core: 2. Of those that a mesh axis runs over, the one named last changes fastest.
Arguments:
- voltages: bfloat16 [2, 256, 8, 65536], P(None, 'beam', 'seg'), may hold values from -6 to 6
- surv_taps: bfloat16 [32], replicated, may hold values from -1 to 1
- ref_taps: bfloat16 [32], replicated, may hold values from -1 to 1
- tx_owner: int32 [4], replicated, may hold values from 0 to 255
- delay_start: int32 [4], replicated, may hold values from 0 to 384
- doppler_start: int32 [4], replicated, may hold values from 0 to 128
Outputs:
- maps: float32 [4, 256, 128, 128], P(None, 'beam', 'seg')
All inputs are finite; a program needn't handle non-finite values.
Results may differ from a plain program's by a relative error of at most 0.0027.
Values may be sent and summed in bfloat16 or wider, within the bound.
A program may use at most 128 MiB of HBM per device.

v0:
```python
import jax
import jax.numpy as jnp
from jax import lax
from jax.sharding import PartitionSpec as P

TX = 4
DECIM = 4
TAPS = 32
BLOCK_LEN = 64
BLOCKS = 256
DELAYS = 128
DOPPLER = 128
MAXDELAY = 512


def from_root(value, axis, source):
    kept = jnp.where(lax.axis_index(axis) == source, value, 0).astype(value.dtype)
    return lax.psum(kept, axis)


def band_matrix(taps):
    rows = DECIM * BLOCK_LEN + TAPS - 1
    row_ids = jnp.arange(rows, dtype=jnp.int32)[:, None]
    col_ids = jnp.arange(BLOCK_LEN, dtype=jnp.int32)[None, :]
    offset = DECIM * col_ids + TAPS - 1 - row_ids
    tap_ids = jnp.arange(TAPS, dtype=jnp.int32)
    picked = jnp.where(offset[..., None] == tap_ids, taps.astype(jnp.float32), 0.0)
    return jnp.sum(picked, axis=-1).astype(jnp.bfloat16)


def decimate(raw, taps):
    lead = raw.shape[:-1]
    stride = DECIM * BLOCK_LEN
    count = raw.shape[-1] // stride
    blocks = raw.reshape(lead + (count, stride))
    tail = blocks[..., :-1, stride - (TAPS - 1) :]
    tail = jnp.pad(tail, [(0, 0)] * len(lead) + [(1, 0), (0, 0)])
    extended = jnp.concatenate([tail, blocks], axis=-1)
    filtered = jnp.einsum(
        "...k,km->...m", extended, band_matrix(taps), preferred_element_type=jnp.float32
    )
    return filtered.astype(jnp.bfloat16).reshape(lead + (count * BLOCK_LEN,))


def tables(f_lo):
    ells = jnp.arange(BLOCKS, dtype=jnp.int32)
    freqs = f_lo + jnp.arange(DOPPLER, dtype=jnp.int32) - BLOCKS // 2
    phase = ells[:, None] * freqs[None, :] % BLOCKS
    angle = 2.0 * jnp.pi / BLOCKS * phase.astype(jnp.float32)
    return (jnp.cos(angle).astype(jnp.bfloat16), jnp.sin(angle).astype(jnp.bfloat16))


def partial_einsum(form, left, right):
    return jnp.einsum(form, left, right, preferred_element_type=jnp.float32)


def ambiguity(surv, ref, d_lo, f_lo):
    beams = surv.shape[1]
    segs = surv.shape[2]
    span = BLOCK_LEN + DELAYS - 1
    extra = (DELAYS - 1 + BLOCK_LEN - 1) // BLOCK_LEN
    cos_t, sin_t = tables(f_lo)
    scale = BLOCK_LEN ** (-0.5)

    def one_segment(seg):
        blocks_s = lax.dynamic_index_in_dim(surv, seg, 2, keepdims=False).reshape(
            2, beams, BLOCKS, BLOCK_LEN
        )
        ref_seg = lax.dynamic_index_in_dim(ref, seg, 1, keepdims=False)
        rpad = jnp.pad(ref_seg, ((0, 0), (MAXDELAY, extra * BLOCK_LEN)))
        start = MAXDELAY - (DELAYS - 1) - d_lo
        rwin = lax.dynamic_slice_in_dim(rpad, start, (BLOCKS + extra) * BLOCK_LEN, 1)
        rwin = rwin.reshape(2, BLOCKS + extra, BLOCK_LEN)
        window = jnp.concatenate([rwin[:, e : e + BLOCKS] for e in range(extra + 1)], axis=2)[
            ..., :span
        ]
        tiled = jnp.tile(window, (1, 1, BLOCK_LEN + 1))[..., : BLOCK_LEN * (span + 1)]
        toeplitz = tiled.reshape(2, BLOCKS, BLOCK_LEN, span + 1)[..., :DELAYS]
        s_re, s_im = (blocks_s[0], blocks_s[1])
        u_re, u_im = (toeplitz[0], toeplitz[1])
        c_re = (
            partial_einsum("blm,lmi->bli", s_re, u_re) + partial_einsum("blm,lmi->bli", s_im, u_im)
        ) * scale
        c_im = (
            partial_einsum("blm,lmi->bli", s_im, u_re) - partial_einsum("blm,lmi->bli", s_re, u_im)
        ) * scale
        c_re = c_re[..., ::-1].astype(jnp.bfloat16)
        c_im = c_im[..., ::-1].astype(jnp.bfloat16)
        x_re = partial_einsum("blj,lf->bjf", c_re, cos_t) + partial_einsum(
            "blj,lf->bjf", c_im, sin_t
        )
        x_im = partial_einsum("blj,lf->bjf", c_im, cos_t) - partial_einsum(
            "blj,lf->bjf", c_re, sin_t
        )
        return (x_re * x_re + x_im * x_im) * (1.0 / (4 * BLOCKS))

    powers = lax.map(one_segment, jnp.arange(segs, dtype=jnp.int32))
    return jnp.sum(powers, axis=0)


def shards(voltages, surv_taps, ref_taps, tx_owner, delay_start, doppler_start):
    beams_here = voltages.shape[1]
    surv = decimate(voltages, surv_taps)
    segments_all = lax.axis_size("seg") * voltages.shape[2]
    collected = []
    for trans in range(TX):
        owner = tx_owner[trans]
        root = owner // beams_here
        local_beam = owner % beams_here
        mine = lax.dynamic_index_in_dim(voltages, local_beam, 1, keepdims=False)
        arrived = from_root(mine, "beam", root)
        ref = decimate(arrived, ref_taps)
        power = ambiguity(surv, ref, delay_start[trans], doppler_start[trans])
        summed = lax.psum_scatter(power, "seg", scatter_dimension=1, tiled=True)
        collected.append(summed / segments_all)
    return jnp.stack(collected, axis=0)


def solution(mesh):
    return jax.shard_map(
        shards,
        mesh=mesh,
        in_specs=(P(None, "beam", "seg", None), P(), P(), P(), P(), P()),
        out_specs=P(None, "beam", "seg", None),
        check_vma=False,
    )
```

profile of v0, /device:TPU:0, one launch (start us, length us, event | category | flops | bytes accessed | tf_op | source)
XLA Modules:
  0.0 667.7 jit_solution(16479196598512230570)
XLA Ops:
  18.5 11.2 %fusion.80 = (bf16[2,65536]{1,0:T(2,128)(2,1)S(1)}, bf16[2,65536]{1,0:T(2,128)(2,1)S(1)}, bf16[2,65536]{1,0:T(2,128)(2,1)S(1)}, bf16[2,65536]{1,0:T(2,128)(2,1)S(1)}) fusion(pred[]{:T(512)S(6)} %eq.30, bf16[2,16,1,65536]{3,1,2,0:T(8,128)(2,1)} %param.6, s32[]{:T(128)S(6)} %select_n.176, s32[]{:T(128)S(6)} %select_n.186, pred[]{:T(512)S(6)} %eq.34, ...), kind=kLoop, calls=%fused_computation.98 | loop fusion | flops 524288 | bytes 2097172 | tf_op jit(solution)/shard_map/jit(_where)/select_n | solution.py:17
  33.9 5.2 copy.157
  39.0 6.3 copy.97
  48.1 3.9 fusion.57
  64.3 91.9 %all-reduce.12.cloned.1.call-done = (bf16[2,1,256,256]{2,3,0,1:T(8,128)(2,1)}, bf16[2,1,256,256]{2,3,0,1:T(8,128)(2,1)}, bf16[2,1,256,256]{2,3,0,1:T(8,128)(2,1)}, bf16[2,1,256,256]{2,3,0,1:T(8,128)(2,1)}) async-done(((bf16[2,1,256,256]{2,3,0,1:T(8,128)(2,1)}, bf16[2,1,256,256]{2,3,0,1:T(8,128)(2,1)}, bf16[2,1,256,256]{2,3,0,1:T(8,128)(2,1)}, bf16[2,1,256,256]{2,3,0,1:T(8,128)(2,1)}), ...) | async-done | bytes 1048592 | tf_op jit(solution)/shard_map/psum | solution.py:18
  162.3 6.2 tile.62
  168.4 14.5 %tile.63 = bf16[2,256,12415]{1,2,0:T(8,128)(2,1)} reshape(bf16[2,256,65,191]{1,3,2,0:T(8,128)(2,1)} %tile.62) | data formatting | bytes 25425920 | tf_op jit(solution)/shard_map/while/body/eval_jaxpr/tile | solution.py:77
  182.9 4.6 slice-done
  187.5 3.7 fusion.256
  191.3 6.7 %copy.155 = bf16[1,256,64,128]{3,2,1,0:T(8,128)(2,1)} copy(bf16[1,256,64,128]{1,3,2,0:T(8,128)(2,1)} %get-tuple-element.90) | data formatting | bytes 8388608
  198.0 4.9 fusion.8
  202.9 2.6 fusion.10
  205.5 6.2 tile.60
  211.6 14.5 %tile.61 = bf16[2,256,12415]{1,2,0:T(8,128)(2,1)} reshape(bf16[2,256,65,191]{1,3,2,0:T(8,128)(2,1)} %tile.60) | data formatting | bytes 25425920 | tf_op jit(solution)/shard_map/while/body/eval_jaxpr/tile | solution.py:77
  226.1 4.6 slice-done.1
  230.7 3.8 fusion.255
  234.5 6.5 copy.153
  241.0 4.9 fusion.16
  245.9 2.6 fusion.18
  249.8 6.2 tile.58
  255.9 14.5 %tile.59 = bf16[2,256,12415]{1,2,0:T(8,128)(2,1)} reshape(bf16[2,256,65,191]{1,3,2,0:T(8,128)(2,1)} %tile.58) | data formatting | bytes 25425920 | tf_op jit(solution)/shard_map/while/body/eval_jaxpr/tile | solution.py:77
  270.4 4.6 slice-done.2
  275.0 3.8 fusion.254
  278.8 6.8 %copy.151 = bf16[1,256,64,128]{3,2,1,0:T(8,128)(2,1)} copy(bf16[1,256,64,128]{1,3,2,0:T(8,128)(2,1)} %get-tuple-element.86) | data formatting | bytes 8388608
  285.6 4.8 fusion.24
  290.4 2.6 fusion.26
  294.3 6.6 copy.154
  300.9 5.6 subtract_bitcast_fusion
  306.5 2.6 add_bitcast_fusion
  309.0 4.1 reverse.30
  313.1 2.8 multiply_convert_fusion.1
  317.5 4.1 reverse.31
  321.7 2.8 multiply_convert_fusion
  324.4 2.4 copy.144
  332.8 7.0 %copy.152 = bf16[1,256,64,128]{3,2,1,0:T(8,128)(2,1)} copy(bf16[1,256,64,128]{1,3,2,0:T(8,128)(2,1)} %get-tuple-element.87) | data formatting | bytes 8388608
  339.8 5.5 subtract_bitcast_fusion.1
  345.3 2.7 add_bitcast_fusion.1
  348.0 4.1 reverse.28
  352.1 2.8 multiply_convert_fusion.3
  356.6 4.2 reverse.29
  360.7 6.6 copy.150
  367.3 5.6 subtract_bitcast_fusion.2
  372.9 2.7 add_bitcast_fusion.2
  375.6 6.2 tile.56
  381.8 14.5 %tile.57 = bf16[2,256,12415]{1,2,0:T(8,128)(2,1)} reshape(bf16[2,256,65,191]{1,3,2,0:T(8,128)(2,1)} %tile.56) | data formatting | bytes 25425920 | tf_op jit(solution)/shard_map/while/body/eval_jaxpr/tile | solution.py:77
  396.3 4.6 slice-done.3
  400.9 3.8 fusion.253
  405.9 2.4 copy.131
  408.3 4.1 reverse.26
  412.4 4.2 reverse.27
  416.6 6.7 %copy.149 = bf16[1,256,64,128]{3,2,1,0:T(8,128)(2,1)} copy(bf16[1,256,64,128]{1,3,2,0:T(8,128)(2,1)} %get-tuple-element.84) | data formatting | bytes 8388608
  423.3 2.3 fusion.152
  430.6 4.7 fusion.34
  435.3 2.8 multiply_convert_fusion.4
  439.7 2.4 copy.118
  442.2 6.6 copy.148
  448.7 5.4 subtract_bitcast_fusion.3
  454.1 4.2 reverse.25
  464.3 4.8 fusion.32
  471.9 5.4 add_bitcast_fusion.3
  477.3 4.1 reverse.24
  489.6 19.4 %reduce-scatter.9.cloned.1.call-done = f32[16,16,128]{2,1,0:T(8,128)} async-done(((f32[16,128,128]{2,1,0:T(8,128)}), f32[16,16,128]{2,1,0:T(8,128)}) %reduce-scatter.9.cloned.1.call-update) | async-done | bytes 131088 | tf_op jit(solution)/shard_map/reduce_scatter | solution.py:114
  510.0 74.1 %reduce-scatter.7.cloned.1.call-done = f32[16,16,128]{2,1,0:T(8,128)} async-done(((f32[16,128,128]{2,1,0:T(8,128)}), f32[16,16,128]{2,1,0:T(8,128)}) %reduce-scatter.7.cloned.1.call-update) | async-done | bytes 131088 | tf_op jit(solution)/shard_map/reduce_scatter | solution.py:114
  585.0 74.2 %reduce-scatter.5.cloned.1.call-done = f32[16,16,128]{2,1,0:T(8,128)} async-done(((f32[16,128,128]{2,1,0:T(8,128)}), f32[16,16,128]{2,1,0:T(8,128)}) %reduce-scatter.5.cloned.1.call-update) | async-done | bytes 131088 | tf_op jit(solution)/shard_map/reduce_scatter | solution.py:114
  (150 shorter events, 61.9 us)
Async XLA Ops:
  6.5 149.7 %all-reduce.12.cloned.1.call-start = ((), (), s32[]{:S(2)}) async-start(), calls=%async_computation.8 | async-start | bytes 2097152 | tf_op jit(solution)/shard_map/psum | solution.py:18
  18.4 15.3 %copy-start.21 = (bf16[32]{0:T(256)(128)(2,1)S(1)}, bf16[32]{0:T(256)(128)(2,1)}, u32[]{:S(2)}) copy-start(bf16[32]{0:T(256)(128)(2,1)} %param.7) | copy-start | bytes 196
  18.5 15.3 %copy-start.22 = (bf16[32]{0:T(256)(128)(2,1)S(1)}, bf16[32]{0:T(256)(128)(2,1)}, u32[]{:S(2)}) copy-start(bf16[32]{0:T(256)(128)(2,1)} %param.8) | copy-start | bytes 196
  33.2 455.5 %reduce-scatter.11.cloned.1.call-start = ((), (), s32[]{:S(2)}) async-start(), calls=%async_computation.7 | async-start | bytes 1179648 | tf_op jit(solution)/shard_map/reduce_scatter | solution.py:114
  48.1 3.9 copy-start.14
  52.0 7.5 %copy-start.15 = (s32[4]{0:T(128)S(1)}, s32[4]{0:T(128)}, u32[]{:S(2)}) copy-start(s32[4]{0:T(128)} %param.11) | copy-start | bytes 52
  182.9 4.6 slice-start
  198.0 4.9 copy-start
  226.1 4.6 slice-start.1
  241.0 4.9 copy-start.1
  245.9 2.6 copy-start.20
  270.4 4.6 slice-start.2
  285.6 4.9 copy-start.2
  290.4 2.6 copy-start.19
  300.9 5.6 copy-start.3
  300.9 5.6 copy-start.11
  326.8 3.1 copy-start.8
  332.8 176.3 %reduce-scatter.9.cloned.1.call-start = ((), (), s32[]{:S(2)}) async-start(), calls=%async_computation.6 | async-start | bytes 1179648 | tf_op jit(solution)/shard_map/reduce_scatter | solution.py:114
  339.8 5.5 copy-start.4
  339.8 5.5 copy-start.9
  367.3 5.6 copy-start.5
  367.3 5.6 copy-start.10
  396.3 4.6 slice-start.3
  400.9 3.8 copy-start.12
  416.6 6.7 %copy-start.18 = (s32[128]{0:T(128)S(1)}, s32[128]{0:T(128)}, u32[]{:S(2)}) copy-start(s32[128]{0:T(128)} %add_add_fusion.1) | copy-start | bytes 1540
  423.3 3.2 copy-start.13
  423.3 4.4 copy-start.6
  435.3 148.8 %reduce-scatter.7.cloned.1.call-start = ((), (), s32[]{:S(2)}) async-start(), calls=%async_computation.5 | async-start | bytes 1179648 | tf_op jit(solution)/shard_map/reduce_scatter | solution.py:114
  454.1 4.2 copy-start.17
  458.3 3.1 copy-start.7
  469.1 190.1 %reduce-scatter.5.cloned.1.call-start = ((), (), s32[]{:S(2)}) async-start(), calls=%async_computation.4 | async-start | bytes 1179648 | tf_op jit(solution)/shard_map/reduce_scatter | solution.py:114
  477.3 6.7 %copy-start.16 = (s32[128]{0:T(128)S(1)}, s32[128]{0:T(128)}, u32[]{:S(2)}) copy-start(s32[128]{0:T(128)} %add_add_fusion.3) | copy-start | bytes 1540
Sparse Core Ops, SparseCore 0:
  33.3 122.8 all-reduce.11
  332.9 73.6 reduce-scatter.10
  435.4 73.5 reduce-scatter.8
  512.5 71.5 reduce-scatter.6
  587.5 71.5 reduce-scatter.4
where the time goes:
time: 678 us; the launch traced here: 668 us
  waiting for transfers between devices  260 us (38%)
  local copies, waits for them, and re-layouts  242 us (36%)
  matrix products  96.6 us (14%)
  other arithmetic  39.1 us (6%)
  between operations  29.2 us (4%)
    reduce_scatter x4, waiting for transfers between devices, shards(): summed = lax.psum_scatter(power, 'seg', scatter_dimension=1, tiled=True)  168 us
    psum x1, waiting for transfers between devices, from_root(): return lax.psum(kept, axis)  91.9 us
    dot_general x32, matrix products, partial_einsum(): return jnp.einsum(form, left, right, preferred_element_type=jnp.float32)  89.7 us
    another operation x8, local copies, waits for them, and re-layouts, one_segment(): jnp.tile(window, (1, 1, BLOCK_LEN + 1))[..., :BLOCK_LEN * (span + 1)]  82.7 us
    unnamed x59, local copies, waits for them, and re-layouts  58.7 us
    another operation x8, local copies, waits for them, and re-layouts  33.2 us
    slice x8, local copies, waits for them, and re-layouts, one_segment(): jnp.tile(window, (1, 1, BLOCK_LEN + 1))[..., :BLOCK_LEN * (span + 1)]  18.3 us
    slice x4, local copies, waits for them, and re-layouts, one_segment(): u_re, u_im = (toeplitz[0], toeplitz[1])  15.1 us
  transfers between devices with their start and end apart: 5, of which 4 were waited for; matrix products, arithmetic and copies ran while one was open for 27% of the time, Pallas kernels for 0%

commit v1 on v0

--- a/solution.py
+++ b/solution.py
@@ -15,7 +15,7 @@
 
 def from_root(value, axis, source):
     kept = jnp.where(lax.axis_index(axis) == source, value, 0).astype(value.dtype)
-    return lax.psum(kept, axis)
+    return jnp.sum(lax.all_gather(kept, axis), axis=0)
 
 
 def band_matrix(taps):

time: 678 us -> 776 us (1.14)
  other arithmetic: 39.1 us -> 162 us
  waiting for transfers between devices: 260 us -> 222 us
  local copies, waits for them, and re-layouts: 242 us -> 264 us
    all_gather x0 -> x4, other arithmetic: none -> 103 us  [from_root(): return jnp.sum(lax.all_gather(kept, axis), axis=0)]
    psum x1 -> x0, waiting for transfers between devices: 91.9 us -> none  [from_root(): return lax.psum(kept, axis)]
    all_gather x0 -> x4, waiting for transfers between devices: none -> 52.4 us  [from_root(): return jnp.sum(lax.all_gather(kept, axis), axis=0)]
    all_gather x0 -> x4, local copies, waits for them, and re-layouts: none -> 25.1 us  [from_root(): return jnp.sum(lax.all_gather(kept, axis), axis=0)]
    reduce_sum x0 -> x4, other arithmetic: none -> 24.1 us  [from_root(): return jnp.sum(lax.all_gather(kept, axis), axis=0)]
    unnamed x59 -> x55, local copies, waits for them, and re-layouts: 58.7 us -> 58.9 us
  transfers between devices with their start and end apart: 5 -> 8, of which waited for: 4 -> 6; matrix products, arithmetic and copies ran while one was open for 27% -> 53% of each run, Pallas kernels for 0% -> 0%
where the time goes in v1:
time: 776 us; the launch traced here: 769 us
  local copies, waits for them, and re-layouts  264 us (34%)
  waiting for transfers between devices  222 us (29%)
  other arithmetic  162 us (21%)
  matrix products  90 us (12%)
  between operations  29.8 us (4%)
    reduce_scatter x4, waiting for transfers between devices, shards(): summed = lax.psum_scatter(power, 'seg', scatter_dimension=1, tiled=True)  168 us
    all_gather x4, other arithmetic, from_root(): return jnp.sum(lax.all_gather(kept, axis), axis=0)  103 us
    dot_general x32, matrix products, partial_einsum(): return jnp.einsum(form, left, right, preferred_element_type=jnp.float32)  85 us
    another operation x8, local copies, waits for them, and re-layouts, one_segment(): jnp.tile(window, (1, 1, BLOCK_LEN + 1))[..., :BLOCK_LEN * (span + 1)]  82.9 us
    unnamed x55, local copies, waits for them, and re-layouts  58.9 us
    all_gather x4, waiting for transfers between devices, from_root(): return jnp.sum(lax.all_gather(kept, axis), axis=0)  52.4 us
    another operation x8, local copies, waits for them, and re-layouts  33.3 us
    all_gather x4, local copies, waits for them, and re-layouts, from_root(): return jnp.sum(lax.all_gather(kept, axis), axis=0)  25.1 us
  transfers between devices with their start and end apart: 8, of which 6 were waited for; matrix products, arithmetic and copies ran while one was open for 53% of the time, Pallas kernels for 0%

profile of v1, /device:TPU:0, one launch (start us, length us, event | category | flops | bytes accessed | tf_op | source)
XLA Modules:
  0.0 769.1 jit_solution(13433049149719868239)
XLA Ops:
  18.5 7.4 broadcast_select_fusion.3
  38.7 5.3 copy.239
  44.0 6.3 copy.165
  53.1 3.9 fusion.57
  59.1 21.4 %all-gather.11.cloned.1.call-done = bf16[32,1,1,65536]{3,2,1,0:T(2,128)(2,1)} async-done(((bf16[2,1,1,65536]{3,2,1,0:T(2,128)(2,1)}), bf16[32,1,1,65536]{3,2,1,0:T(2,128)(2,1)}) %all-gather.11.cloned.1.call-update) | async-done | bytes 4194320 | tf_op jit(solution)/shard_map/all_gather | solution.py:18
  80.6 25.9 %reduce.13 = bf16[32,65536]{1,0:T(8,128)(2,1)} reduce(bf16[32,1,1,65536]{3,2,1,0:T(2,128)(2,1)} %all-gather.11.cloned.1.call-done, bf16[]{:T(256)} %constant.253), dimensions={1,2}, to_apply=%all-gather.1.reduce_sub_computation | reduce | bytes 8388610 | tf_op jit(solution)/shard_map/all_gather | solution.py:18
  106.4 6.3 reshape.281
  112.7 6.0 reduce.9
  118.9 16.4 %all-gather.15.cloned.1.call-done = bf16[32,1,1,65536]{3,2,1,0:T(2,128)(2,1)} async-done(((bf16[2,1,1,65536]{3,2,1,0:T(2,128)(2,1)}), bf16[32,1,1,65536]{3,2,1,0:T(2,128)(2,1)}) %all-gather.15.cloned.1.call-update) | async-done | bytes 4194320 | tf_op jit(solution)/shard_map/all_gather | solution.py:18
  135.3 25.8 %reduce.15 = bf16[32,65536]{1,0:T(8,128)(2,1)} reduce(bf16[32,1,1,65536]{3,2,1,0:T(2,128)(2,1)} %all-gather.15.cloned.1.call-done, bf16[]{:T(256)} %constant.253), dimensions={1,2}, to_apply=%all-gather.3.reduce_sub_computation | reduce | bytes 8388610 | tf_op jit(solution)/shard_map/all_gather | solution.py:18
  161.0 6.7 reshape.283
  167.7 6.0 reduce.11
  175.4 14.6 %all-gather.13.cloned.1.call-done = bf16[32,1,1,65536]{3,2,1,0:T(2,128)(2,1)} async-done(((bf16[2,1,1,65536]{3,2,1,0:T(2,128)(2,1)}), bf16[32,1,1,65536]{3,2,1,0:T(2,128)(2,1)}) %all-gather.13.cloned.1.call-update) | async-done | bytes 4194320 | tf_op jit(solution)/shard_map/all_gather | solution.py:18
  190.0 25.8 %reduce.14 = bf16[32,65536]{1,0:T(8,128)(2,1)} reduce(bf16[32,1,1,65536]{3,2,1,0:T(2,128)(2,1)} %all-gather.13.cloned.1.call-done, bf16[]{:T(256)} %constant.253), dimensions={1,2}, to_apply=%all-gather.2.reduce_sub_computation | reduce | bytes 8388610 | tf_op jit(solution)/shard_map/all_gather | solution.py:18
  215.8 6.1 reshape.282
  221.9 6.0 reduce.10
  230.6 6.2 tile.62
  236.8 14.6 %tile.63 = bf16[2,256,12415]{1,2,0:T(8,128)(2,1)} reshape(bf16[2,256,65,191]{1,3,2,0:T(8,128)(2,1)} %tile.62) | data formatting | bytes 25425920 | tf_op jit(solution)/shard_map/while/body/eval_jaxpr/tile | solution.py:77
  251.4 4.6 slice-done
  255.9 3.8 fusion.252
  259.7 6.5 copy.237
  266.2 6.2 tile.58
  272.4 14.7 %tile.59 = bf16[2,256,12415]{1,2,0:T(8,128)(2,1)} reshape(bf16[2,256,65,191]{1,3,2,0:T(8,128)(2,1)} %tile.58) | data formatting | bytes 25425920 | tf_op jit(solution)/shard_map/while/body/eval_jaxpr/tile | solution.py:77
  287.1 4.6 slice-done.1
  291.6 3.8 fusion.250
  295.4 6.6 copy.231
  302.0 6.2 tile.60
  308.1 14.5 %tile.61 = bf16[2,256,12415]{1,2,0:T(8,128)(2,1)} reshape(bf16[2,256,65,191]{1,3,2,0:T(8,128)(2,1)} %tile.60) | data formatting | bytes 25425920 | tf_op jit(solution)/shard_map/while/body/eval_jaxpr/tile | solution.py:77
  322.6 4.6 slice-done.2
  327.2 3.7 fusion.251
  330.9 6.9 copy.234
  337.9 4.9 fusion.8
  355.6 25.8 %reduce.12 = bf16[32,65536]{1,0:T(8,128)(2,1)} reduce(bf16[32,1,1,65536]{3,2,1,0:T(2,128)(2,1)} %all-gather.9.cloned.1.call-done, bf16[]{:T(256)} %constant.253), dimensions={1,2}, to_apply=%all-gather.reduce_sub_computation | reduce | bytes 8388610 | tf_op jit(solution)/shard_map/all_gather | solution.py:18
  381.4 6.1 reshape.280
  387.5 6.0 reduce.8
  394.9 6.6 copy.236
  401.5 5.6 subtract_bitcast_fusion
  409.7 4.2 reverse.30
  418.3 4.2 reverse.31
  433.7 6.8 copy.230
  440.5 5.5 subtract_bitcast_fusion.2
  448.7 4.1 reverse.26
  452.8 2.8 multiply_convert_fusion.5
  457.2 4.2 reverse.27
  461.4 6.6 copy.233
  468.0 5.6 subtract_bitcast_fusion.1
  476.3 6.2 tile.56
  482.4 14.5 %tile.57 = bf16[2,256,12415]{1,2,0:T(8,128)(2,1)} reshape(bf16[2,256,65,191]{1,3,2,0:T(8,128)(2,1)} %tile.56) | data formatting | bytes 25425920 | tf_op jit(solution)/shard_map/while/body/eval_jaxpr/tile | solution.py:77
  496.9 4.6 slice-done.3
  501.5 3.8 fusion.249
  508.9 4.1 reverse.28
  513.0 4.2 reverse.29
  517.2 6.9 copy.228
  531.5 4.7 fusion.34
  536.3 2.8 multiply_convert_fusion.2
  543.1 6.5 copy.227
  549.6 5.4 subtract_bitcast_fusion.3
  555.0 4.2 reverse.25
  565.2 4.8 fusion.32
  572.8 5.4 add_bitcast_fusion.3
  578.2 4.1 reverse.24
  590.5 19.4 %reduce-scatter.7.cloned.1.call-done = f32[16,16,128]{2,1,0:T(8,128)} async-done(((f32[16,128,128]{2,1,0:T(8,128)}), f32[16,16,128]{2,1,0:T(8,128)}) %reduce-scatter.7.cloned.1.call-update) | async-done | bytes 131088 | tf_op jit(solution)/shard_map/reduce_scatter | solution.py:114
  610.8 74.3 %reduce-scatter.9.cloned.1.call-done = f32[16,16,128]{2,1,0:T(8,128)} async-done(((f32[16,128,128]{2,1,0:T(8,128)}), f32[16,16,128]{2,1,0:T(8,128)}) %reduce-scatter.9.cloned.1.call-update) | async-done | bytes 131088 | tf_op jit(solution)/shard_map/reduce_scatter | solution.py:114
  686.0 74.3 %reduce-scatter.5.cloned.1.call-done = f32[16,16,128]{2,1,0:T(8,128)} async-done(((f32[16,128,128]{2,1,0:T(8,128)}), f32[16,16,128]{2,1,0:T(8,128)}) %reduce-scatter.5.cloned.1.call-update) | async-done | bytes 131088 | tf_op jit(solution)/shard_map/reduce_scatter | solution.py:114
  (167 shorter events, 93.1 us)
Async XLA Ops:
  6.5 21.8 %copy-start.14 = (s32[4]{0:T(128)S(1)}, s32[4]{0:T(128)}, u32[]{:S(2)}) copy-start(s32[4]{0:T(128)} %param.10) | copy-start | bytes 52
  6.5 27.3 %copy-start.19 = (bf16[32]{0:T(256)(128)(2,1)S(1)}, bf16[32]{0:T(256)(128)(2,1)}, u32[]{:S(2)}) copy-start(bf16[32]{0:T(256)(128)(2,1)} %param.7) | copy-start | bytes 196
  6.5 27.3 %copy-start.20 = (bf16[32]{0:T(256)(128)(2,1)S(1)}, bf16[32]{0:T(256)(128)(2,1)}, u32[]{:S(2)}) copy-start(bf16[32]{0:T(256)(128)(2,1)} %param.8) | copy-start | bytes 196
  6.5 27.4 %copy-start.15 = (s32[4]{0:T(128)S(1)}, s32[4]{0:T(128)}, u32[]{:S(2)}) copy-start(s32[4]{0:T(128)} %param.11) | copy-start | bytes 52
  6.5 74.0 %all-gather.11.cloned.1.call-start = ((), (), s32[]{:S(2)}) async-start(), calls=%async_computation.9 | async-start | bytes 8912896 | tf_op jit(solution)/shard_map/all_gather | solution.py:18
  25.9 109.4 %all-gather.15.cloned.1.call-start = ((), (), s32[]{:S(2)}) async-start(), calls=%async_computation.11 | async-start | bytes 8912896 | tf_op jit(solution)/shard_map/all_gather | solution.py:18
  26.6 163.4 %all-gather.13.cloned.1.call-start = ((), (), s32[]{:S(2)}) async-start(), calls=%async_computation.10 | async-start | bytes 8912896 | tf_op jit(solution)/shard_map/all_gather | solution.py:18
  27.4 328.2 %all-gather.9.cloned.1.call-start = ((), (), s32[]{:S(2)}) async-start(), calls=%async_computation.8 | async-start | bytes 8912896 | tf_op jit(solution)/shard_map/all_gather | solution.py:18
  27.9 561.6 %reduce-scatter.11.cloned.1.call-start = ((), (), s32[]{:S(2)}) async-start(), calls=%async_computation.7 | async-start | bytes 1179648 | tf_op jit(solution)/shard_map/reduce_scatter | solution.py:114
  251.4 4.6 slice-start
  287.1 4.6 slice-start.1
  322.6 4.6 slice-start.2
  337.9 4.9 copy-start
  342.7 2.6 copy-start.1
  347.9 2.6 copy-start.2
  401.5 5.6 copy-start.3
  401.5 5.6 copy-start.11
  427.7 3.1 copy-start.8
  433.7 176.2 %reduce-scatter.7.cloned.1.call-start = ((), (), s32[]{:S(2)}) async-start(), calls=%async_computation.5 | async-start | bytes 1179648 | tf_op jit(solution)/shard_map/reduce_scatter | solution.py:114
  440.5 5.6 copy-start.4
  440.5 5.6 copy-start.10
  467.9 5.6 copy-start.5
  467.9 5.6 copy-start.9
  496.9 4.6 slice-start.3
  501.5 3.8 copy-start.12
  517.2 7.0 copy-start.18
  524.2 3.2 copy-start.13
  524.2 4.5 copy-start.6
  536.2 148.9 %reduce-scatter.9.cloned.1.call-start = ((), (), s32[]{:S(2)}) async-start(), calls=%async_computation.6 | async-start | bytes 1179648 | tf_op jit(solution)/shard_map/reduce_scatter | solution.py:114
  555.0 4.2 copy-start.17
  559.2 3.1 copy-start.7
  570.0 190.3 %reduce-scatter.5.cloned.1.call-start = ((), (), s32[]{:S(2)}) async-start(), calls=%async_computation.4 | async-start | bytes 1179648 | tf_op jit(solution)/shard_map/reduce_scatter | solution.py:114
  578.2 6.7 copy-start.16
Sparse Core Ops, SparseCore 0:
  26.0 54.5 all-gather.10
  82.3 52.9 all-gather.14
  137.0 52.9 all-gather.12
  191.6 52.9 all-gather.8
  433.8 73.5 reduce-scatter.10
  536.4 73.4 reduce-scatter.6
  613.5 71.5 reduce-scatter.8
  688.7 71.5 reduce-scatter.4
